TPU v7x, 128 devices: a whole 4x4x4 slice. The times are simulated.
128 devices in a mesh: row: 8 (over x_hi, y), col: 16 (over z, x_lo, core).
Axes of the slice: x: 4 (x_hi: 2, x_lo: 2; x = x_hi * 2 + x_lo), y: 4, z: 4, core: 2. Of those that a mesh axis runs over, the one named last changes fastest.
Arguments:
- lower_left: float32 [12288, 16384], P('row', 'col'), may hold values from -0.0546875 to 0.0546875
- lower_cotan: float32 [12288, 16384], P('row', 'col'), may hold values from -6 to 6
- panel: float32 [12288, 512], P('row', 'col'), may hold values from -0.0546875 to 0.0546875
- panel_cotan: float32 [12288, 512], P('row', 'col'), may hold values from -6 to 6
- diag_factor: float32 [512, 512], P('row', 'col'), as said below
- inverse_factor: float32 [512, 512], P('row', 'col'), as said below
- diag_cotan: float32 [512, 512], P('row', 'col'), may hold values from -6 to 6
- row_factor: float32 [512, 16384], P('row', 'col'), may hold values from -0.25 to 0.25
- row_cotan: float32 [512, 16384], P('row', 'col'), may hold values from -6 to 6
Outputs:
- lower_grad: float32 [12288, 16384], P('row', 'col')
- panel_grad: float32 [12288, 512], P('row', 'col')
- diag_grad: float32 [512, 512], P('row', 'col')
- row_grad: float32 [512, 16384], P('row', 'col')
Inputs may be any that keep to these rules, and one draw needn't show every extreme that they name: diag_factor is lower triangular with a positive diagonal, and inverse_factor is its inverse. inverse_factor is the inverse of diag_factor, lower triangular.
All inputs are finite; a program needn't handle non-finite values.
Results may differ from a plain program's by a relative error of at most 0.00016.
Values sent between devices are 32-bit elements; how exact they have to be, the bound alone decides.
No kernel may reach another device: no remote copies, remote signals or barrier semaphores. Data moves between devices by JAX's collectives and lax.ppermute only.
A program may use at most 128 MiB of HBM per device.

v0:
```python
import jax
import jax.numpy as jnp
from jax import lax
from jax.sharding import PartitionSpec as P


def product(left, right):
    return jnp.dot(left, right, precision=lax.Precision.HIGHEST, preferred_element_type=jnp.float32)


def lower_half(matrix):
    return jnp.tril(matrix) - 0.5 * jnp.diag(jnp.diag(matrix))


def local(
    lower_left,
    lower_cotan,
    panel,
    panel_cotan,
    diag_factor,
    inverse_factor,
    diag_cotan,
    row_factor,
    row_cotan,
):
    n_rows = lax.axis_size("row")
    n_cols = lax.axis_size("col")
    row_pos = lax.axis_index("row")
    col_pos = lax.axis_index("col")
    nb_row = diag_factor.shape[0]
    nb_col = diag_factor.shape[1]
    width = nb_row * n_rows
    stacked = (
        lax.all_gather(diag_factor[None], ("row", "col"), axis=0, tiled=True),
        lax.all_gather(inverse_factor[None], ("row", "col"), axis=0, tiled=True),
        lax.all_gather(diag_cotan[None], ("row", "col"), axis=0, tiled=True),
    )

    def assemble(stack):
        return (
            stack.reshape(n_rows, n_cols, nb_row, nb_col)
            .transpose(0, 2, 1, 3)
            .reshape(width, width)
        )

    full_factor = assemble(stacked[0])
    full_inverse = assemble(stacked[1])
    full_cotan = assemble(stacked[2])
    cotan_rows = lax.all_gather(panel_cotan, "col", axis=1, tiled=True)
    solved = product(cotan_rows, full_inverse)
    panel_rows = lax.all_gather(panel, "col", axis=1, tiled=True)
    summed = lax.psum(product(solved.T, panel_rows), "row")
    diag_step = full_cotan - jnp.tril(summed)
    inner = lower_half(product(full_factor.T, diag_step))
    diag_full = lower_half(product(product(full_inverse.T, inner), full_inverse))
    both = diag_full + diag_full.T
    diag_grad = lax.dynamic_slice(diag_full, (row_pos * nb_row, col_pos * nb_col), (nb_row, nb_col))
    panel_grad = lax.dynamic_slice_in_dim(solved, col_pos * nb_col, nb_col, 1)
    both_rows = lax.dynamic_slice_in_dim(both, row_pos * nb_row, nb_row, 0)
    piece = lax.all_gather(row_factor, "row", axis=0, tiled=True)
    lower_acc = lower_cotan
    left = solved
    lower_acc = lower_acc - product(left, piece)
    row_acc = product(both_rows, piece)
    left = solved
    term = product(left.T, lower_left)
    cross_part = lax.psum_scatter(term, "row", scatter_dimension=0, tiled=True)
    row_grad = row_cotan - cross_part - row_acc
    return (lower_acc, panel_grad, diag_grad, row_grad)


def solution(mesh):
    placed = (
        P("row", "col"),
        P("row", "col"),
        P("row", "col"),
        P("row", "col"),
        P("row", "col"),
        P("row", "col"),
        P("row", "col"),
        P("row", "col"),
        P("row", "col"),
    )
    return jax.shard_map(
        local,
        mesh=mesh,
        in_specs=placed,
        out_specs=(P("row", "col"), P("row", "col"), P("row", "col"), P("row", "col")),
        check_vma=False,
    )
```

profile of v0, /device:TPU:0, one launch (start us, length us, event | category | flops | bytes accessed | tf_op | source)
XLA Modules:
  0.0 904.5 jit_solution(6461293442693684772)
XLA Ops:
  7.2 0.0 all-gather.19.cloned.1.call-start
  7.2 0.7 all-gather.19.cloned.1.call-update
  7.9 0.0 all-gather.13.cloned.1.call-start
  7.9 0.7 all-gather.13.cloned.1.call-update
  8.6 0.0 all-gather.17.cloned.1.call-start
  8.7 0.7 all-gather.17.cloned.1.call-update
  9.4 0.0 all-gather.23.cloned.1.call-start
  9.4 0.5 all-gather.23.cloned.1.call-update
  10.0 0.0 all-gather.21.cloned.1.call-start
  10.0 0.5 all-gather.21.cloned.1.call-update
  10.5 0.0 all-gather.15.cloned.1.call-start
  10.6 0.5 all-gather.15.cloned.1.call-update
  11.1 0.0 all-reduce.2.cloned.1.call-start
  11.2 197.0 %all-gather.19.cloned.1.call-done = f32[128,64,32]{1,2,0:T(8,128)} async-done(((f32[1,64,32]{1,2,0:T(8,128)}), f32[128,64,32]{1,2,0:T(8,128)}) %all-gather.19.cloned.1.call-update) | async-done | bytes 1048592 | tf_op jit(solution)/shard_map/all_gather | solution.py:35
  208.2 3.2 copy.39
  211.4 1.5 reshape.29
  212.9 30.9 %all-gather.13.cloned.1.call-done = f32[1536,512]{0,1:T(8,128)} async-done(((f32[1536,32]{0,1:T(8,128)}), f32[1536,512]{0,1:T(8,128)}) %all-gather.13.cloned.1.call-update) | async-done | bytes 3145744 | tf_op jit(solution)/shard_map/all_gather | solution.py:49
  243.8 7.4 fusion.29
  251.2 29.8 %all-gather.17.cloned.1.call-done = f32[1536,512]{0,1:T(8,128)} async-done(((f32[1536,32]{0,1:T(8,128)}), f32[1536,512]{0,1:T(8,128)}) %all-gather.17.cloned.1.call-update) | async-done | bytes 3145744 | tf_op jit(solution)/shard_map/all_gather | solution.py:51
  281.0 7.5 fusion.30
  288.5 0.0 all-reduce.2.cloned.1.call-update
  288.6 0.2 reduce-scatter.2.cloned.1.call-start
  288.8 13.2 %fusion.32 = f32[512,1024]{1,0:T(8,128)} fusion(f32[1536,512]{0,1:T(8,128)S(1)} %fusion.29, f32[1536,1024]{1,0:T(8,128)} %param.9), kind=kOutput, calls=%fused_computation.45 | convolution fusion | flops 9663676416 | bytes 11534336 | tf_op jit(solution)/shard_map/dot_general | solution.py:8
  302.0 0.0 reduce-scatter.2.cloned.1.call-update
  302.0 176.4 %all-gather.23.cloned.1.call-done = f32[128,64,32]{1,2,0:T(8,128)} async-done(((f32[1,64,32]{1,2,0:T(8,128)}), f32[128,64,32]{1,2,0:T(8,128)}) %all-gather.23.cloned.1.call-update) | async-done | bytes 1048592 | tf_op jit(solution)/shard_map/all_gather | solution.py:34
  478.5 4.5 copy.37
  483.0 2.7 reshape.33
  485.7 188.7 %all-gather.21.cloned.1.call-done = f32[128,64,32]{1,2,0:T(8,128)} async-done(((f32[1,64,32]{1,2,0:T(8,128)}), f32[128,64,32]{1,2,0:T(8,128)}) %all-gather.21.cloned.1.call-update) | async-done | bytes 1048592 | tf_op jit(solution)/shard_map/all_gather | solution.py:36
  674.4 4.5 copy.38
  678.9 2.8 reshape.31
  681.7 2.6 copy.28
  684.2 0.7 constant_dynamic-slice_fusion
  684.9 43.4 %all-gather.15.cloned.1.call-done = f32[512,1024]{1,0:T(8,128)} async-done(((f32[64,1024]{1,0:T(8,128)}), f32[512,1024]{1,0:T(8,128)}) %all-gather.15.cloned.1.call-update) | async-done | bytes 2097168 | tf_op jit(solution)/shard_map/all_gather | solution.py:60
  728.3 14.1 %convolution_subtract_fusion = f32[1536,1024]{1,0:T(8,128)} fusion(f32[1536,1024]{1,0:T(8,128)} %param.10, f32[1536,512]{0,1:T(8,128)S(1)} %fusion.29, f32[512,1024]{1,0:T(8,128)} %all-gather.15.cloned.1.call-done), kind=kOutput, calls=%fused_computation.2 | convolution fusion | flops 9665249280 | bytes 17825792 | tf_op jit(solution)/shard_map/dot_general | solution.py:8
  742.4 74.1 %all-reduce.2.cloned.1.call-done = f32[512,512]{1,0:T(8,128)} async-done(((f32[512,512]{1,0:T(8,128)}), f32[512,512]{1,0:T(8,128)}) %all-reduce.2.cloned.1.call-update) | async-done | bytes 1048592 | tf_op jit(solution)/shard_map/psum | solution.py:52
  816.5 3.7 convolution_bitcast_fusion
  820.3 4.5 gather_fusion
  824.8 2.4 fusion
  827.2 1.9 fusion.31
  829.1 0.0 copy-start.3
  829.1 4.5 gather_fusion.1
  833.7 1.3 copy.31
  835.0 1.4 multiply_subtract_fusion
  836.4 1.0 copy-done.2
  837.4 0.1 dynamic_slice.10
  837.5 0.7 copy.32
  838.1 56.4 %reduce-scatter.2.cloned.1.call-done = f32[64,1024]{1,0:T(8,128)} async-done(((f32[512,1024]{1,0:T(8,128)}), f32[64,1024]{1,0:T(8,128)}) %reduce-scatter.2.cloned.1.call-update) | async-done | bytes 262160 | tf_op jit(solution)/shard_map/reduce_scatter | solution.py:67
  894.5 3.1 convolution_subtract_fusion.1
  (7 shorter events, 0.0 us)
Async XLA Ops:
  7.2 201.0 %all-gather.19.cloned.1.call-start = ((), (), s32[]{:S(2)}) async-start(), calls=%async_computation.6 | async-start | bytes 2113536 | tf_op jit(solution)/shard_map/all_gather | solution.py:35
  7.9 235.9 %all-gather.13.cloned.1.call-start = ((), (), s32[]{:S(2)}) async-start(), calls=%async_computation.1 | async-start | bytes 3342336 | tf_op jit(solution)/shard_map/all_gather | solution.py:49
  8.6 272.4 %all-gather.17.cloned.1.call-start = ((), (), s32[]{:S(2)}) async-start(), calls=%async_computation.3 | async-start | bytes 3342336 | tf_op jit(solution)/shard_map/all_gather | solution.py:51
  9.4 469.1 %all-gather.23.cloned.1.call-start = ((), (), s32[]{:S(2)}) async-start(), calls=%async_computation.8 | async-start | bytes 2113536 | tf_op jit(solution)/shard_map/all_gather | solution.py:34
  10.0 664.4 %all-gather.21.cloned.1.call-start = ((), (), s32[]{:S(2)}) async-start(), calls=%async_computation.7 | async-start | bytes 2113536 | tf_op jit(solution)/shard_map/all_gather | solution.py:36
  10.5 717.8 %all-gather.15.cloned.1.call-start = ((), (), s32[]{:S(2)}) async-start(), calls=%async_computation.2 | async-start | bytes 2359296 | tf_op jit(solution)/shard_map/all_gather | solution.py:60
  11.1 805.4 %all-reduce.2.cloned.1.call-start = ((), (), s32[]{:S(2)}) async-start(), calls=%async_computation.4 | async-start | bytes 2097152 | tf_op jit(solution)/shard_map/psum | solution.py:52
  288.6 606.0 %reduce-scatter.2.cloned.1.call-start = ((), (), s32[]{:S(2)}) async-start(), calls=%async_computation.5 | async-start | bytes 2359296 | tf_op jit(solution)/shard_map/reduce_scatter | solution.py:67
  742.4 82.4 %copy-start = (f32[512,512]{0,1:T(8,128)S(1)}, f32[512,512]{0,1:T(8,128)}, u32[]{:S(2)}) copy-start(f32[512,512]{0,1:T(8,128)} %reshape.29) | copy-start | bytes 3145732
  829.1 65.4 %copy-start.1 = (f32[512,1024]{1,0:T(8,128)S(1)}, f32[512,1024]{1,0:T(8,128)}, u32[]{:S(2)}) copy-start(f32[512,1024]{1,0:T(8,128)} %all-gather.15.cloned.1.call-done) | copy-start | bytes 6291460
  829.1 65.4 %copy-start.3 = (f32[64,1024]{1,0:T(8,128)S(1)}, f32[64,1024]{1,0:T(8,128)}, u32[]{:S(2)}) copy-start(f32[64,1024]{1,0:T(8,128)} %param.17) | copy-start | bytes 786436
  836.4 1.0 copy-start.2
Sparse Core Ops, SparseCore 0:
  9.7 198.4 all-gather.18
  209.9 33.8 all-gather.12
  245.5 35.4 all-gather.16
  282.6 195.8 all-gather.22
  480.0 194.2 all-gather.20
  676.6 51.7 all-gather.14
  730.8 85.6 all-reduce.1
  820.3 74.2 reduce-scatter.1
where the time goes:
time: 905 us; the launch traced here: 904 us
  waiting for transfers between devices  800 us (88%)
  matrix products  53.4 us (6%)
  local copies, waits for them, and re-layouts  34.7 us (4%)
  between operations  14.2 us (2%)
    all_gather x1, waiting for transfers between devices, local(): lax.all_gather(inverse_factor[None], ('row', 'col'), axis=0, tiled=True)  197 us
    all_gather x1, waiting for transfers between devices, local(): lax.all_gather(diag_cotan[None], ('row', 'col'), axis=0, tiled=True)  189 us
    all_gather x1, waiting for transfers between devices, local(): lax.all_gather(diag_factor[None], ('row', 'col'), axis=0, tiled=True)  176 us
    psum x1, waiting for transfers between devices, local(): summed = lax.psum(product(solved.T, panel_rows), 'row')  74.1 us
    reduce_scatter x1, waiting for transfers between devices, local(): cross_part = lax.psum_scatter(term, 'row', scatter_dimension=0, tiled=True)  56.4 us
    dot_general x8, matrix products, product(): jnp.dot(left, right, precision=lax.Precision.HIGHEST, preferred_element_t...  53.4 us
    all_gather x1, waiting for transfers between devices, local(): piece = lax.all_gather(row_factor, 'row', axis=0, tiled=True)  43.4 us
    all_gather x1, waiting for transfers between devices, local(): cotan_rows = lax.all_gather(panel_cotan, 'col', axis=1, tiled=True)  30.9 us
  transfers between devices with their start and end apart: 8, of which 8 were waited for; matrix products, arithmetic and copies ran while one was open for 9% of the time, Pallas kernels for 0%

commit v1 on v0

v1 whole, which is shorter than its diff:
```python
import jax
import jax.numpy as jnp
from jax import lax
from jax.experimental import pallas as pl
from jax.experimental.pallas import tpu as pltpu
from jax.sharding import PartitionSpec as P


X_HI, Y, Z, X_LO, CORE = 2, 4, 4, 2, 2
ROWS, COLS = X_HI * Y, Z * X_LO * CORE
BOTH = ("row", "col")
F32, BF16 = jnp.float32, jnp.bfloat16
AT_ROW, MY_ROW, MY_COL = 16, 24, 25


def shift(value, x_hi=0, y=0, z=0, x_lo=0, core=0):
    pairs = []
    for r in range(ROWS):
        for c in range(COLS):
            r2 = (r // Y + x_hi) % X_HI * Y + (r % Y + y) % Y
            c2 = (c // 4 + z) % Z * 4 + (c // 2 + x_lo) % X_LO * 2 + (c + core) % CORE
            pairs.append((r * COLS + c, r2 * COLS + c2))
    return lax.ppermute(value, BOTH, pairs)


def ring4(value, axis):
    return [value] + [shift(value, **{axis: -s if s < 3 else 1}) for s in (1, 2, 3)]


def after(value, *others):
    return lax.optimization_barrier((value,) + others)[0]


def split(value):
    high = value.astype(BF16)
    return high, (value - high.astype(F32)).astype(BF16)


def dot(a, b, ca=1, cb=0):
    return lax.dot_general(a, b, (((ca,), (cb,)), ((), ())), preferred_element_type=F32)


def dot_high(a, b, ca, cb):
    return lax.dot_general(
        a, b, (((ca,), (cb,)), ((), ())), precision=lax.Precision.HIGH, preferred_element_type=F32
    )


def dot3(a, b, ca=1, cb=0):
    return dot(a[0], b[0], ca, cb) + (dot(a[0], b[1], ca, cb) + dot(a[1], b[0], ca, cb))


def call(body, table, args, out_shapes, flops, scratch=(), far=0, limit=16):
    vmem, hbm = pl.BlockSpec(memory_space=pltpu.VMEM), pl.BlockSpec(memory_space=pltpu.HBM)
    size = sum(a.size * a.dtype.itemsize for a in list(args) + list(out_shapes))
    return pl.pallas_call(
        body,
        out_shape=out_shapes,
        in_specs=[pl.BlockSpec(memory_space=pltpu.SMEM)] + [hbm] * far + [vmem] * (len(args) - far),
        out_specs=[vmem] * len(out_shapes),
        scratch_shapes=list(scratch),
        compiler_params=pltpu.CompilerParams(vmem_limit_bytes=limit << 20),
        cost_estimate=pl.CostEstimate(flops=int(flops), bytes_accessed=int(size), transcendentals=0),
    )(table, *args)


def fetch(pairs, sems):
    copies = [pltpu.make_async_copy(src, dst, sems.at[n]) for n, (src, dst) in enumerate(pairs)]
    for copy in copies:
        copy.start()
    for copy in copies:
        copy.wait()


def out(shape, dtype=F32):
    return jax.ShapeDtypeStruct(shape, dtype)


def unpack_body(tab, *refs):
    extra, cotan, tall = refs[8:]
    for n, piece in enumerate(refs[:8]):
        tall[pl.ds(pl.multiple_of(tab[AT_ROW + n] * 64, 64), 64), :] = piece[...]
    flat = tall[...].T
    extra[...] = flat[0:64, :]
    cotan[...] = flat[64:96, :]


def chain_body(tab, e0, e1, e2, e3, sums, cotan, inv_t, stepped, res, fac_t):
    for f, s, d in ((f, s, d) for f in range(2) for s in range(4) for d in range(2)):
        piece = ((e0, e1), (e2, e3))[f][d]
        at = pl.ds(pl.multiple_of(tab[f * 8 + s * 2 + d] * 32, 32), 32)
        inv_t[at, :] = piece[s, 0:32, :]
        fac_t[at, :] = piece[s, 32:64, :]
    for n in range(8):
        at = pl.ds(pl.multiple_of(tab[AT_ROW + n] * 64, 64), 64)
        stepped[n * 64 : n * 64 + 64, :] = inv_t[at, :]
    total = sums[0]
    for r in range(1, ROWS):
        total = total + sums[r]
    inverse = split(inv_t[...].T)
    j = lax.broadcasted_iota(jnp.int32, (32, 512), 1)
    c = lax.broadcasted_iota(jnp.int32, (32, 512), 0) + tab[MY_COL] * 32
    step = cotan[...] - jnp.where(j >= c, dot3(split(total), inverse), 0.0)
    inner = dot3(split(step), split(fac_t[...].T))
    inner = jnp.where(j > c, inner, jnp.where(j == c, 0.5 * inner, 0.0))
    x = dot3(split(inner), inverse)
    for r in range(COLS):
        res[r] = x


def near_body(tab, *refs):
    res = refs[8]
    for n, piece in enumerate(refs[:8]):
        res[pl.ds(pl.multiple_of((tab[n] >> 1) * 32, 32), 32), :] = piece[...]


def panel_body(tab, near, far, res):
    core = tab[MY_COL] & 1
    for n in range(8):
        at = n * 32
        res[pl.ds(pl.multiple_of((n * 2 + core) * 32, 32), 32), :] = near[at : at + 32, :]
        res[pl.ds(pl.multiple_of((n * 2 + 1 - core) * 32, 32), 32), :] = far[at : at + 32, :]


def rows_body(tab, *refs):
    res, sems = refs[8:]
    pairs = []
    for n, piece in enumerate(refs[:8]):
        at = pl.ds(pl.multiple_of(tab[AT_ROW + n] * 64, 64), 64)
        pairs.append((piece, res.at[at]))
    fetch(pairs, sems)


def tail_body(tab, kept_far, come_far, cotan_far, rows_far, inv_far, xs, mine, row, diag, kept, come, cotan, rows, inv_t, sems):
    fars, nears = (inv_far, rows_far, kept_far, come_far, cotan_far), (inv_t, rows, kept, come, cotan)
    copies = [pltpu.make_async_copy(src, dst, sems.at[n]) for n, (src, dst) in enumerate(zip(fars, nears))]
    for copy in copies:
        copy.start()
    x = split(xs[...])
    copies[0].wait()
    high = dot3(split(inv_t[pl.ds(pl.multiple_of(tab[MY_ROW] * 64, 64), 64), :]), x)
    i = lax.broadcasted_iota(jnp.int32, (512, 64), 0)
    j = lax.broadcasted_iota(jnp.int32, (512, 64), 1) + tab[MY_ROW] * 64
    pick = jnp.where(i == j, 1.0, 0.0).astype(BF16)
    x_rows = (dot(x[0], pick).astype(BF16), dot(x[1], pick).astype(BF16))
    low_t = dot3(split(inv_t[...]), x_rows)
    corner_t = dot3(split(mine[...]), x_rows)
    i = lax.broadcasted_iota(jnp.int32, (64, 512), 0) + tab[MY_ROW] * 64
    j = lax.broadcasted_iota(jnp.int32, (64, 512), 1)
    both = split(jnp.where(i >= j, low_t.T, high))
    for copy in copies[1:]:
        copy.wait()
    row[...] = cotan[...] - (kept[...] + come[...]) - dot3(both, split(rows[...]))
    i = lax.broadcasted_iota(jnp.int32, (32, 64), 1) + tab[MY_ROW] * 64
    j = lax.broadcasted_iota(jnp.int32, (32, 64), 0) + tab[MY_COL] * 32
    diag[...] = jnp.where(i > j, corner_t, jnp.where(i == j, 0.5 * corner_t, 0.0)).T


def local(
    lower_left,
    lower_cotan,
    panel,
    panel_cotan,
    diag_factor,
    inverse_factor,
    diag_cotan,
    row_factor,
    row_cotan,
):
    row_pos = lax.axis_index("row")
    col_pos = lax.axis_index("col")
    x_hi, y = row_pos >> 2, row_pos & 3
    z, x_lo, core = col_pos >> 2, (col_pos >> 1) & 1, col_pos & 1
    q = lax.iota(jnp.int32, 32)
    table = (((z + (q >> 1)) & 3) << 2) + ((x_lo ^ (q & 1)) << 1) + (core ^ (q >> 3))
    table = jnp.where(q >= AT_ROW, ((x_hi ^ (q & 1)) << 2) + ((y + ((q - AT_ROW) >> 1)) & 3), table)
    table = jnp.where(q == MY_ROW, row_pos, jnp.where(q == MY_COL, col_pos, table))

    mine = panel_cotan.T
    other = shift(mine, x_lo=1)
    mine3, mine1 = shift(mine, z=1), shift(mine, z=-1)
    other3, other1 = shift(other, z=1), shift(other, z=-1)
    mine2 = shift(mine3, z=1)
    other2 = shift(other1, z=-1)
    near = [mine, other, mine1, other1, mine2, other2, mine3, other3]
    half = call(near_body, table, near, (out((256, 1536)),), 1e5)[0]
    far = shift(half, core=1)
    a_t = call(panel_body, table, (half, far), (out((512, 1536)),), 1e5)[0]

    def over_row(mine):
        other = shift(mine, x_hi=1)
        mine3, mine1 = shift(mine, y=1), shift(mine, y=-1)
        other3, other1 = shift(other, y=1), shift(other, y=-1)
        mine2, other2 = shift(mine3, y=1), shift(other1, y=-1)
        return mine, other, mine1, other1, mine2, other2, mine3, other3

    pad = jnp.zeros((64, 32), F32)
    s_parts = over_row(jnp.concatenate([inverse_factor, diag_factor, diag_cotan, pad], 1))
    r_parts = over_row(row_factor)

    sums = dot_high(panel, a_t, 0, 1)
    sums = jnp.broadcast_to(sums[None], (ROWS, 32, 512))
    gathered = lax.all_to_all(sums, "row", 0, 0, tiled=True)
    cross = dot_high(after(a_t, sums), lower_left, 1, 0)

    extra, cotan_t = call(
        unpack_body, table, s_parts, (out((64, 512)), out((32, 512))), 1e5, scratch=(pltpu.VMEM((512, 128), F32),)
    )
    e0 = jnp.stack(ring4(extra, "z"))
    e2 = shift(e0, core=1)
    e1 = shift(e0, x_lo=1)
    e3 = shift(e1, core=1)
    inv_t, stepped, x_mine = call(
        chain_body, table, (e0, e1, e2, e3, gathered, cotan_t),
        (out((512, 512)), out((512, 512)), out((COLS, 32, 512))), 4e8, scratch=(pltpu.VMEM((512, 512), F32),),
    )
    x_t = lax.all_to_all(x_mine, "col", 0, 0, tiled=True).reshape(512, 512)

    turned = dot_high(stepped, cross, 1, 0).reshape(Y, 2, 64, -1)
    up, down = shift(turned[2, 0], y=1), shift(turned[2, 1], y=-1)
    up = shift(jnp.stack([turned[1, 0] + up, turned[1, 1]]), y=1)
    down = shift(jnp.stack([turned[3, 0], turned[3, 1] + down]), y=-1)
    come = shift(turned[0, 1] + up[1] + down[1], x_hi=1)
    kept = turned[0, 0] + up[0] + down[0]

    r_full = call(
        rows_body, table, r_parts, (out((512, 1024)),), 1e5, scratch=(pltpu.SemaphoreType.DMA((8,)),), far=8
    )[0]

    spread = dot_high(inv_t, r_full, 0, 0)
    lower_grad = lower_cotan - dot_high(a_t, spread, 0, 0)
    panel_grad = dot_high(a_t, extra[:32], 0, 1)
    row_grad, diag_grad = call(
        tail_body, table, (kept, come, row_cotan, r_full, inv_t, x_t, extra[:32]),
        (out((64, 1024)), out((64, 32))), 4e8,
        scratch=(pltpu.VMEM((64, 1024), F32),) * 3
        + (pltpu.VMEM((512, 1024), F32), pltpu.VMEM((512, 512), F32), pltpu.SemaphoreType.DMA((5,))), far=5, limit=56,
    )
    return (lower_grad, panel_grad, diag_grad, row_grad)


def solution(mesh):
    placed = (P("row", "col"),) * 9

    return jax.shard_map(local, mesh=mesh, in_specs=placed, out_specs=(P("row", "col"),) * 4, check_vma=False)
```

time: 905 us -> 157 us (0.17)
  waiting for transfers between devices: 800 us -> 34 us
  starting transfers between devices: 0.49 us -> 65.2 us
  matrix products: 53.4 us -> 26.2 us
  local copies, waits for them, and re-layouts: 34.7 us -> 11.6 us
  Pallas kernels: 0 us -> 13.3 us
  between operations: 14.2 us -> 0.9 us
    all_gather x6 -> x0, waiting for transfers between devices: 666 us -> none  [the longest x1 197 us: local(): lax.all_gather(inverse_factor[None], ('row', 'col'), axis=0, tiled=True)]
    psum x1 -> x0, waiting for transfers between devices: 74.1 us -> none  [local(): summed = lax.psum(product(solved.T, panel_rows), 'row')]
    ppermute x0 -> x33, starting transfers between devices: none -> 56.5 us  [shift(): return lax.ppermute(value, BOTH, pairs)]
    reduce_scatter x1 -> x0, waiting for transfers between devices: 56.4 us -> none  [local(): cross_part = lax.psum_scatter(term, 'row', scatter_dimension=0, tiled=True)]
    ppermute x0 -> x33, waiting for transfers between devices: none -> 34 us  [shift(): return lax.ppermute(value, BOTH, pairs)]
    dot_general x8 -> x6, matrix products: 53.4 us -> 26.2 us  [dot_high(): lax.dot_general(a, b, (((ca,), (cb,)), ((), ())), precision=lax.Precision...]
    reshape x7 -> x0, local copies, waits for them, and re-layouts: 21.9 us -> none  [the longest x3 12.3 us: assemble(): stack.reshape(n_rows, n_cols, nb_row, nb_col).transpose(0, 2, 1, 3)]
    pallas_call x0 -> x6, Pallas kernels: none -> 13.3 us  [call(): pl.pallas_call(body, out_shape=out_shapes, in_specs=[pl.BlockSpec(memory_...]
  transfers between devices with their start and end apart: 8 -> 35, of which waited for: 8 -> 15; matrix products, arithmetic and copies ran while one was open for 9% -> 21% of each run, Pallas kernels for 0% -> 4%
where the time goes in v1:
time: 157 us; the launch traced here: 156 us
  starting transfers between devices  65.2 us (42%)
  waiting for transfers between devices  34 us (22%)
  matrix products  26.2 us (17%)
  Pallas kernels  13.3 us (8%)
  local copies, waits for them, and re-layouts  11.6 us (7%)
  other arithmetic  4.93 us (3%)
    ppermute x33, starting transfers between devices, shift(): return lax.ppermute(value, BOTH, pairs)  56.5 us
    ppermute x33, waiting for transfers between devices, shift(): return lax.ppermute(value, BOTH, pairs)  34 us
    dot_general x6, matrix products, dot_high(): lax.dot_general(a, b, (((ca,), (cb,)), ((), ())), precision=lax.Precision...  26.2 us
    pallas_call x6, Pallas kernels, call(): pl.pallas_call(body, out_shape=out_shapes, in_specs=[pl.BlockSpec(memory_...  13.3 us
    unnamed x36, local copies, waits for them, and re-layouts  9.92 us
    all_to_all x1, starting transfers between devices, local(): x_t = lax.all_to_all(x_mine, 'col', 0, 0, tiled=True).reshape(512, 512)  4.35 us
    all_to_all x1, starting transfers between devices, local(): gathered = lax.all_to_all(sums, 'row', 0, 0, tiled=True)  4.34 us
  transfers between devices with their start and end apart: 35, of which 15 were waited for; matrix products, arithmetic and copies ran while one was open for 21% of the time, Pallas kernels for 4%

profile of v1, /device:TPU:0, one launch (start us, length us, event | category | flops | bytes accessed | tf_op | source)
XLA Modules:
  0.0 156.1 jit_solution(6345993334158983020)
XLA Ops:
  0.7 1.7 %collective-permute-start = (f32[32,1536]{1,0:T(8,128)}, f32[32,1536]{1,0:T(8,128)S(1)}, u32[]{:S(2)}, u32[]{:S(2)}) collective-permute-start(f32[32,1536]{1,0:T(8,128)} %bitcast.73), channel_id=1, source_target_pairs={{0,2},{1,3},{2,0},{3,1},{4,6},{5,7},{6,4},{7,5},{8,10},{9,11},{10,... | collective-permute-start | bytes 589832 | tf_op jit(solution)/shard_map/ppermute | solution.py:23
  2.3 1.9 %collective-permute-start.3 = (f32[32,1536]{1,0:T(8,128)}, f32[32,1536]{1,0:T(8,128)S(1)}, u32[]{:S(2)}, u32[]{:S(2)}) collective-permute-start(f32[32,1536]{1,0:T(8,128)} %bitcast.74), channel_id=1, source_target_pairs={{0,4},{1,5},{2,6},{3,7},{4,8},{5,9},{6,10},{7,11},{8,12},{9,13},{1... | collective-permute-start | bytes 589832 | tf_op jit(solution)/shard_map/ppermute | solution.py:23
  4.3 3.2 %collective-permute-done.refs_1_ = f32[32,1536]{1,0:T(8,128)S(1)} collective-permute-done((f32[32,1536]{1,0:T(8,128)}, f32[32,1536]{1,0:T(8,128)S(1)}, u32[]{:S(2)}, u32[]{:S(2)}) %collective-permute-start) | collective-permute-done | bytes 196640 | tf_op jit(solution)/shard_map/ppermute | solution.py:23
  7.5 4.3 %collective-permute-start.2 = (f32[32,1536]{1,0:T(8,128)S(1)}, f32[32,1536]{1,0:T(8,128)S(1)}, u32[]{:S(2)}, u32[]{:S(2)}) collective-permute-start(f32[32,1536]{1,0:T(8,128)S(1)} %collective-permute-done.refs_1_), channel_id=1, source_target_pairs={{0,12},{1,13},{2,14},{3,15},{4,0},{5,1},{6,2},{7,3},{8,4},{9,5},{1... | collective-permute-start | bytes 589832 | tf_op jit(solution)/shard_map/ppermute | solution.py:23
  12.1 1.6 %collective-permute-start.6 = (f32[32,1536]{1,0:T(8,128)S(1)}, f32[32,1536]{1,0:T(8,128)S(1)}, u32[]{:S(2)}, u32[]{:S(2)}) collective-permute-start(f32[32,1536]{1,0:T(8,128)S(1)} %collective-permute-done.refs_1_), channel_id=1, source_target_pairs={{0,4},{1,5},{2,6},{3,7},{4,8},{5,9},{6,10},{7,11},{8,12},{9,13},{1... | collective-permute-start | bytes 589832 | tf_op jit(solution)/shard_map/ppermute | solution.py:23
  13.8 3.2 %collective-permute-done.2.refs_3_ = f32[32,1536]{1,0:T(8,128)S(1)} collective-permute-done((f32[32,1536]{1,0:T(8,128)S(1)}, f32[32,1536]{1,0:T(8,128)S(1)}, u32[]{:S(2)}, u32[]{:S(2)}) %collective-permute-start.2) | collective-permute-done | bytes 196640 | tf_op jit(solution)/shard_map/ppermute | solution.py:23
  17.0 3.7 %collective-permute-start.5 = (f32[32,1536]{1,0:T(8,128)S(1)}, f32[32,1536]{1,0:T(8,128)S(1)}, u32[]{:S(2)}, u32[]{:S(2)}) collective-permute-start(f32[32,1536]{1,0:T(8,128)S(1)} %collective-permute-done.2.refs_3_), channel_id=1, source_target_pairs={{0,12},{1,13},{2,14},{3,15},{4,0},{5,1},{6,2},{7,3},{8,4},{9,5},{1... | collective-permute-start | bytes 589832 | tf_op jit(solution)/shard_map/ppermute | solution.py:23
  21.4 1.4 collective-permute-done.4.refs_4_
  22.8 1.1 collective-permute-done.5.refs_5_
  26.0 3.1 %collective-permute-start.8 = (f32[64,128]{1,0:T(8,128)S(1)}, f32[64,128]{1,0:T(8,128)S(1)}, u32[]{:S(2)}, u32[]{:S(2)}) collective-permute-start(f32[64,128]{1,0:T(8,128)S(1)} %maximum_maximum_fusion.refs_0_), channel_id=1, source_target_pairs={{0,64},{1,65},{2,66},{3,67},{4,68},{5,69},{6,70},{7,71},{8,72},{9,... | collective-permute-start | bytes 98312 | tf_op jit(solution)/shard_map/ppermute | solution.py:23
  29.1 1.6 %collective-permute-start.11 = (f32[64,128]{1,0:T(8,128)S(1)}, f32[64,128]{1,0:T(8,128)S(1)}, u32[]{:S(2)}, u32[]{:S(2)}) collective-permute-start(f32[64,128]{1,0:T(8,128)S(1)} %maximum_maximum_fusion.refs_0_), channel_id=1, source_target_pairs={{0,16},{1,17},{2,18},{3,19},{4,20},{5,21},{6,22},{7,23},{8,24},{9,... | collective-permute-start | bytes 98312 | tf_op jit(solution)/shard_map/ppermute | solution.py:23
  31.5 3.0 %collective-permute-start.10 = (f32[64,128]{1,0:T(8,128)S(1)}, f32[64,128]{1,0:T(8,128)S(1)}, u32[]{:S(2)}, u32[]{:S(2)}) collective-permute-start(f32[64,128]{1,0:T(8,128)S(1)} %collective-permute-done.8.refs_1_), channel_id=1, source_target_pairs={{0,48},{1,49},{2,50},{3,51},{4,52},{5,53},{6,54},{7,55},{8,56},{9,... | collective-permute-start | bytes 98312 | tf_op jit(solution)/shard_map/ppermute | solution.py:23
  35.3 1.3 collective-permute-start.14
  36.6 3.2 %collective-permute-start.13 = (f32[64,128]{1,0:T(8,128)S(1)}, f32[64,128]{1,0:T(8,128)S(1)}, u32[]{:S(2)}, u32[]{:S(2)}) collective-permute-start(f32[64,128]{1,0:T(8,128)S(1)} %collective-permute-done.10.refs_3_), channel_id=1, source_target_pairs={{0,48},{1,49},{2,50},{3,51},{4,52},{5,53},{6,54},{7,55},{8,56},{9,... | collective-permute-start | bytes 98312 | tf_op jit(solution)/shard_map/ppermute | solution.py:23
  40.4 1.3 collective-permute-done.12.refs_4_
  42.4 3.8 %collective-permute-start.15 = (f32[64,512]{1,0:T(8,128)S(1)}, f32[64,512]{1,0:T(8,128)S(1)}, u32[]{:S(2)}, u32[]{:S(2)}) collective-permute-start(f32[64,512]{1,0:T(8,128)S(1)} %get-tuple-element.12), channel_id=1, source_target_pairs={{0,12},{1,13},{2,14},{3,15},{4,0},{5,1},{6,2},{7,3},{8,4},{9,5},{1... | collective-permute-start | bytes 393224 | tf_op jit(solution)/shard_map/ppermute | solution.py:23
  47.1 3.0 %collective-permute-done.15 = f32[64,512]{1,0:T(8,128)S(1)} collective-permute-done((f32[64,512]{1,0:T(8,128)S(1)}, f32[64,512]{1,0:T(8,128)S(1)}, u32[]{:S(2)}, u32[]{:S(2)}) %collective-permute-start.15) | collective-permute-done | bytes 131104 | tf_op jit(solution)/shard_map/ppermute | solution.py:23
  50.1 2.6 %collective-permute-done.16 = f32[64,512]{1,0:T(8,128)S(1)} collective-permute-done((f32[64,512]{1,0:T(8,128)S(1)}, f32[64,512]{1,0:T(8,128)S(1)}, u32[]{:S(2)}, u32[]{:S(2)}) %collective-permute-start.16) | collective-permute-done | bytes 131104 | tf_op jit(solution)/shard_map/ppermute | solution.py:23
  54.6 1.5 collective-permute-start.18
  56.1 2.7 %collective-permute-start.21 = (f32[64,1024]{1,0:T(8,128)}, f32[64,1024]{1,0:T(8,128)}, u32[]{:S(2)}, u32[]{:S(2)}) collective-permute-start(f32[64,1024]{1,0:T(8,128)} %refs_0_.1), channel_id=1, source_target_pairs={{0,64},{1,65},{2,66},{3,67},{4,68},{5,69},{6,70},{7,71},{8,72},{9,... | collective-permute-start | bytes 786440 | tf_op jit(solution)/shard_map/ppermute | solution.py:23
  59.0 3.1 %collective-permute-start.22 = (f32[64,1024]{1,0:T(8,128)}, f32[64,1024]{1,0:T(8,128)}, u32[]{:S(2)}, u32[]{:S(2)}) collective-permute-start(f32[64,1024]{1,0:T(8,128)} %refs_0_.1), channel_id=1, source_target_pairs={{0,48},{1,49},{2,50},{3,51},{4,52},{5,53},{6,54},{7,55},{8,56},{9,... | collective-permute-start | bytes 786440 | tf_op jit(solution)/shard_map/ppermute | solution.py:23
  62.1 10.4 %collective-permute-done.21.refs_1_ = f32[64,1024]{1,0:T(8,128)} collective-permute-done((f32[64,1024]{1,0:T(8,128)}, f32[64,1024]{1,0:T(8,128)}, u32[]{:S(2)}, u32[]{:S(2)}) %collective-permute-start.21) | collective-permute-done | bytes 262176 | tf_op jit(solution)/shard_map/ppermute | solution.py:23
  72.5 3.0 %collective-permute-start.23 = (f32[64,1024]{1,0:T(8,128)}, f32[64,1024]{1,0:T(8,128)}, u32[]{:S(2)}, u32[]{:S(2)}) collective-permute-start(f32[64,1024]{1,0:T(8,128)} %collective-permute-done.21.refs_1_), channel_id=1, source_target_pairs={{0,48},{1,49},{2,50},{3,51},{4,52},{5,53},{6,54},{7,55},{8,56},{9,... | collective-permute-start | bytes 786440 | tf_op jit(solution)/shard_map/ppermute | solution.py:23
  75.5 1.2 copy-done.5
  76.9 1.4 copy-done.3
  78.3 1.4 copy-done.6
  80.4 1.5 convolution_bitcast_fusion
  82.8 4.3 %all-to-all-start = ((f32[8,32,512]{2,1,0:T(8,128)}), f32[8,32,512]{2,1,0:T(8,128)}, u32[]{:S(2)}, u32[]{:S(2)}) async-start(f32[8,32,512]{2,1,0:T(8,128)} %broadcast_in_dim.19), calls=%async_computation | async-start | bytes 1048576 | tf_op jit(solution)/shard_map/all_to_all | solution.py:203
  87.1 8.2 %fusion.11 = f32[512,1024]{1,0:T(8,128)} fusion(f32[512,1536]{1,0:T(8,128)S(1)} %shard_map.121, f32[1536,1024]{1,0:T(8,128)} %param.9), kind=kOutput, calls=%fused_computation.32 | convolution fusion | flops 4831838208 | bytes 11534336 | tf_op jit(solution)/shard_map/dot_general | solution.py:44
  95.4 1.7 %collective-permute-start.27 = (f32[64,1024]{1,0:T(8,128)}, f32[64,1024]{1,0:T(8,128)}, u32[]{:S(2)}, u32[]{:S(2)}) collective-permute-start(f32[64,1024]{1,0:T(8,128)} %collective-permute-done.21.refs_1_), channel_id=1, source_target_pairs={{0,16},{1,17},{2,18},{3,19},{4,20},{5,21},{6,22},{7,23},{8,24},{9,... | collective-permute-start | bytes 786440 | tf_op jit(solution)/shard_map/ppermute | solution.py:23
  97.1 1.5 collective-permute-start.25
  98.6 1.8 %collective-permute-start.26 = (f32[64,1024]{1,0:T(8,128)}, f32[64,1024]{1,0:T(8,128)}, u32[]{:S(2)}, u32[]{:S(2)}) collective-permute-start(f32[64,1024]{1,0:T(8,128)} %collective-permute-done.23.refs_3_), channel_id=1, source_target_pairs={{0,48},{1,49},{2,50},{3,51},{4,52},{5,53},{6,54},{7,55},{8,56},{9,... | collective-permute-start | bytes 786440 | tf_op jit(solution)/shard_map/ppermute | solution.py:23
  100.3 3.3 %shard_map.123 = (f32[512,512]{1,0:T(8,128)S(1)}, f32[512,512]{1,0:T(8,128)S(1)}, f32[16,32,512]{2,1,0:T(8,128)S(1)}) custom-call(s32[32]{0:T(128)S(1)} %compare_select_fusion.2.tab, f32[4,64,512]{2,1,0:T(8,128)} %pad_maximum_fusion.e0, f32[4,64,512]{2,1,0:T(8,128)} %collective-permute-done.18.e1, f32[4,64,512]{2,1,0:T(8,128)} %collective-permute-done.19.e2, ...), custom_call_target="tpu_custom_call" | custom-call | flops 400000000 | bytes 5832704 | tf_op jit(solution)/shard_map/pallas_call | solution.py:56
  105.6 1.9 %fusion.12 = f32[512,1024]{1,0:T(8,128)S(1)} fusion(f32[512,512]{1,0:T(8,128)S(1)} %get-tuple-element.15, f32[512,1024]{1,0:T(8,128)S(1)} %copy-done.12), kind=kOutput, calls=%fused_computation.33 | convolution fusion | flops 1610612736 | bytes 5242880 | tf_op jit(solution)/shard_map/dot_general | solution.py:44
  107.9 3.0 %collective-permute-start.30 = (f32[64,1024]{1,0:T(8,128)S(1)}, f32[64,1024]{1,0:T(8,128)S(1)}, u32[]{:S(2)}, u32[]{:S(2)}) collective-permute-start(f32[64,1024]{1,0:T(8,128)S(1)} %get-tuple-element.29), channel_id=1, source_target_pairs={{0,48},{1,49},{2,50},{3,51},{4,52},{5,53},{6,54},{7,55},{8,56},{9,... | collective-permute-start | bytes 786440 | tf_op jit(solution)/shard_map/ppermute | solution.py:23
  111.6 2.1 %shard_map.124.rows_far = f32[512,1024]{1,0:T(8,128)S(1)} custom-call(s32[32]{0:T(128)S(1)} %compare_select_fusion.2.tab, f32[64,1024]{1,0:T(8,128)S(1)} %copy-done.8, f32[64,1024]{1,0:T(8,128)} %collective-permute-done.21.refs_1_, f32[64,1024]{1,0:T(8,128)} %collective-permute-done.22.refs_2_, f32[64,1024]{1,0:T(8,128)} %collective-permute-done.23.refs_3_, ...), custom_call_target="tpu_custom_call" | custom-call | flops 100000 | bytes 4194304 | tf_op jit(solution)/shard_map/pallas_call | solution.py:56
  113.6 1.3 copy-done.1
  115.0 1.6 collective-permute-done.28
  118.5 3.0 %collective-permute-start.31 = (f32[2,64,1024]{2,1,0:T(8,128)}, f32[2,64,1024]{2,1,0:T(8,128)}, u32[]{:S(2)}, u32[]{:S(2)}) collective-permute-start(f32[2,64,1024]{2,1,0:T(8,128)} %pad_maximum_fusion.2), channel_id=1, source_target_pairs={{0,48},{1,49},{2,50},{3,51},{4,52},{5,53},{6,54},{7,55},{8,56},{9,... | collective-permute-start | bytes 1572872 | tf_op jit(solution)/shard_map/ppermute | solution.py:23
  121.5 1.7 %fusion.8 = f32[1536,32]{0,1:T(8,128)} fusion(f32[512,1536]{1,0:T(8,128)S(1)} %shard_map.121, f32[64,512]{1,0:T(8,128)S(1)} %get-tuple-element.12), kind=kOutput, calls=%fused_computation.29 | convolution fusion | flops 150994944 | bytes 3407872 | tf_op jit(solution)/shard_map/dot_general | solution.py:44
  123.2 4.4 %all-to-all-start.1 = ((f32[16,32,512]{2,1,0:T(8,128)}), f32[16,32,512]{2,1,0:T(8,128)}, u32[]{:S(2)}, u32[]{:S(2)}) async-start(f32[16,32,512]{2,1,0:T(8,128)} %copy-done.7), calls=%async_computation.1 | async-start | bytes 2097152 | tf_op jit(solution)/shard_map/all_to_all | solution.py:217
  127.5 3.8 %fusion.10 = f32[512,1024]{1,0:T(8,128)S(1)} fusion(f32[512,512]{1,0:T(8,128)} %copy-done.4, f32[512,1024]{1,0:T(8,128)} %copy-done.1), kind=kOutput, calls=%fused_computation.31 | convolution fusion | flops 1610612736 | bytes 5242880 | tf_op jit(solution)/shard_map/dot_general | solution.py:44
  131.5 2.2 %fusion = (f32[64,1024]{1,0:T(8,128)}, f32[64,1024]{1,0:T(8,128)}) fusion(f32[2,64,1024]{2,1,0:T(8,128)} %collective-permute-done.31, f32[2,64,1024]{2,1,0:T(8,128)} %collective-permute-done.29, f32[4,2,64,1024]{3,2,1,0:T(8,128)} %bitcast.79), kind=kLoop, calls=%fused_computation.6 | loop fusion | flops 262144 | bytes 2097152 | tf_op jit(solution)/shard_map/add | solution.py:223
  133.7 3.0 %collective-permute-start.32 = (f32[64,1024]{1,0:T(8,128)}, f32[64,1024]{1,0:T(8,128)}, u32[]{:S(2)}, u32[]{:S(2)}) collective-permute-start(f32[64,1024]{1,0:T(8,128)} %get-tuple-element.24), channel_id=1, source_target_pairs={{0,64},{1,65},{2,66},{3,67},{4,68},{5,69},{6,70},{7,71},{8,72},{9,... | collective-permute-start | bytes 786440 | tf_op jit(solution)/shard_map/ppermute | solution.py:23
  136.7 9.2 %convolution_subtract_fusion = f32[1536,1024]{1,0:T(8,128)} fusion(f32[1536,1024]{1,0:T(8,128)} %param.10, f32[512,1536]{1,0:T(8,128)S(1)} %shard_map.121, f32[512,1024]{1,0:T(8,128)S(1)} %fusion.10), kind=kOutput, calls=%fused_computation | convolution fusion | flops 4833411072 | bytes 17825792 | tf_op jit(solution)/shard_map/dot_general | solution.py:44
  145.9 2.9 %collective-permute-done.32.come_far = f32[64,1024]{1,0:T(8,128)} collective-permute-done((f32[64,1024]{1,0:T(8,128)}, f32[64,1024]{1,0:T(8,128)}, u32[]{:S(2)}, u32[]{:S(2)}) %collective-permute-start.32) | collective-permute-done | bytes 262176 | tf_op jit(solution)/shard_map/ppermute | solution.py:23
  148.8 5.9 %shard_map.125 = (f32[64,1024]{1,0:T(8,128)}, f32[64,32]{1,0:T(8,128)}) custom-call(s32[32]{0:T(128)} %copy-done.10, f32[64,1024]{1,0:T(8,128)} %get-tuple-element.25.kept_far, f32[64,1024]{1,0:T(8,128)} %collective-permute-done.32.come_far, f32[64,1024]{1,0:T(8,128)} %cotan_far.1, f32[512,1024]{1,0:T(8,128)} %copy-done.1, f32[512,512]{1,0:T(8,128)} %copy-done.4, ...), custom_call_target="tpu_custom_call" | custom-call | flops 400000000 | bytes 5316608 | tf_op jit(solution)/shard_map/pallas_call | solution.py:56
  154.7 1.4 copy.16
  (82 shorter events, 16.0 us)
Async XLA Ops:
  0.6 79.8 %copy-start = (f32[1536,32]{0,1:T(8,128)S(1)}, f32[1536,32]{0,1:T(8,128)}, u32[]{:S(2)}) copy-start(f32[1536,32]{0,1:T(8,128)} %param.11) | copy-start | bytes 589828
  0.6 25.0 %copy-start.13 = (f32[64,32]{0,1:T(8,128)S(1)}, f32[64,32]{0,1:T(8,128)}, u32[]{:S(2)}) copy-start(f32[64,32]{0,1:T(8,128)} %param.14) | copy-start | bytes 24580
  0.7 6.8 %collective-permute-start = (f32[32,1536]{1,0:T(8,128)}, f32[32,1536]{1,0:T(8,128)S(1)}, u32[]{:S(2)}, u32[]{:S(2)}) collective-permute-start(f32[32,1536]{1,0:T(8,128)} %bitcast.73), channel_id=1, source_target_pairs={{0,2},{1,3},{2,0},{3,1},{4,6},{5,7},{6,4},{7,5},{8,10},{9,11},{10,... | collective-permute-start | bytes 589832 | tf_op jit(solution)/shard_map/ppermute | solution.py:23
  2.3 11.4 %collective-permute-start.3 = (f32[32,1536]{1,0:T(8,128)}, f32[32,1536]{1,0:T(8,128)S(1)}, u32[]{:S(2)}, u32[]{:S(2)}) collective-permute-start(f32[32,1536]{1,0:T(8,128)} %bitcast.74), channel_id=1, source_target_pairs={{0,4},{1,5},{2,6},{3,7},{4,8},{5,9},{6,10},{7,11},{8,12},{9,13},{1... | collective-permute-start | bytes 589832 | tf_op jit(solution)/shard_map/ppermute | solution.py:23
  7.5 9.6 %collective-permute-start.2 = (f32[32,1536]{1,0:T(8,128)S(1)}, f32[32,1536]{1,0:T(8,128)S(1)}, u32[]{:S(2)}, u32[]{:S(2)}) collective-permute-start(f32[32,1536]{1,0:T(8,128)S(1)} %collective-permute-done.refs_1_), channel_id=1, source_target_pairs={{0,12},{1,13},{2,14},{3,15},{4,0},{5,1},{6,2},{7,3},{8,4},{9,5},{1... | collective-permute-start | bytes 589832 | tf_op jit(solution)/shard_map/ppermute | solution.py:23
  11.7 9.6 %collective-permute-start.1 = (f32[32,1536]{1,0:T(8,128)}, f32[32,1536]{1,0:T(8,128)S(1)}, u32[]{:S(2)}, u32[]{:S(2)}) collective-permute-start(f32[32,1536]{1,0:T(8,128)} %bitcast.75), channel_id=1, source_target_pairs={{0,12},{1,13},{2,14},{3,15},{4,0},{5,1},{6,2},{7,3},{8,4},{9,5},{1... | collective-permute-start | bytes 589832 | tf_op jit(solution)/shard_map/ppermute | solution.py:23
  12.1 9.2 %collective-permute-start.6 = (f32[32,1536]{1,0:T(8,128)S(1)}, f32[32,1536]{1,0:T(8,128)S(1)}, u32[]{:S(2)}, u32[]{:S(2)}) collective-permute-start(f32[32,1536]{1,0:T(8,128)S(1)} %collective-permute-done.refs_1_), channel_id=1, source_target_pairs={{0,4},{1,5},{2,6},{3,7},{4,8},{5,9},{6,10},{7,11},{8,12},{9,13},{1... | collective-permute-start | bytes 589832 | tf_op jit(solution)/shard_map/ppermute | solution.py:23
  13.8 9.0 %collective-permute-start.4 = (f32[32,1536]{1,0:T(8,128)S(1)}, f32[32,1536]{1,0:T(8,128)S(1)}, u32[]{:S(2)}, u32[]{:S(2)}) collective-permute-start(f32[32,1536]{1,0:T(8,128)S(1)} %collective-permute-done.3.refs_6_), channel_id=1, source_target_pairs={{0,4},{1,5},{2,6},{3,7},{4,8},{5,9},{6,10},{7,11},{8,12},{9,13},{1... | collective-permute-start | bytes 589832 | tf_op jit(solution)/shard_map/ppermute | solution.py:23
  17.0 6.9 %collective-permute-start.5 = (f32[32,1536]{1,0:T(8,128)S(1)}, f32[32,1536]{1,0:T(8,128)S(1)}, u32[]{:S(2)}, u32[]{:S(2)}) collective-permute-start(f32[32,1536]{1,0:T(8,128)S(1)} %collective-permute-done.2.refs_3_), channel_id=1, source_target_pairs={{0,12},{1,13},{2,14},{3,15},{4,0},{5,1},{6,2},{7,3},{8,4},{9,5},{1... | collective-permute-start | bytes 589832 | tf_op jit(solution)/shard_map/ppermute | solution.py:23
  20.7 90.8 %copy-start.10 = (s32[32]{0:T(128)}, s32[32]{0:T(128)S(1)}, u32[]{:S(2)}) copy-start(s32[32]{0:T(128)S(1)} %compare_select_fusion.2.tab) | copy-start | bytes 388
  25.5 50.0 %copy-start.2 = (f32[256,1536]{1,0:T(8,128)}, f32[256,1536]{1,0:T(8,128)S(1)}, u32[]{:S(2)}) copy-start(f32[256,1536]{1,0:T(8,128)S(1)} %shard_map.120.near) | copy-start | bytes 4718596
  25.5 49.9 %collective-permute-start.7 = (f32[256,1536]{1,0:T(8,128)S(1)}, f32[256,1536]{1,0:T(8,128)S(1)}, u32[]{:S(2)}, u32[]{:S(2)}) collective-permute-start(f32[256,1536]{1,0:T(8,128)S(1)} %shard_map.120.near), channel_id=1, source_target_pairs={{0,1},{1,0},{2,3},{3,2},{4,5},{5,4},{6,7},{7,6},{8,9},{9,8},{10,11... | collective-permute-start | bytes 4718600 | tf_op jit(solution)/shard_map/ppermute | solution.py:23
  26.0 5.5 %collective-permute-start.8 = (f32[64,128]{1,0:T(8,128)S(1)}, f32[64,128]{1,0:T(8,128)S(1)}, u32[]{:S(2)}, u32[]{:S(2)}) collective-permute-start(f32[64,128]{1,0:T(8,128)S(1)} %maximum_maximum_fusion.refs_0_), channel_id=1, source_target_pairs={{0,64},{1,65},{2,66},{3,67},{4,68},{5,69},{6,70},{7,71},{8,72},{9,... | collective-permute-start | bytes 98312 | tf_op jit(solution)/shard_map/ppermute | solution.py:23
  29.1 7.4 %collective-permute-start.11 = (f32[64,128]{1,0:T(8,128)S(1)}, f32[64,128]{1,0:T(8,128)S(1)}, u32[]{:S(2)}, u32[]{:S(2)}) collective-permute-start(f32[64,128]{1,0:T(8,128)S(1)} %maximum_maximum_fusion.refs_0_), channel_id=1, source_target_pairs={{0,16},{1,17},{2,18},{3,19},{4,20},{5,21},{6,22},{7,23},{8,24},{9,... | collective-permute-start | bytes 98312 | tf_op jit(solution)/shard_map/ppermute | solution.py:23
  31.5 5.1 %collective-permute-start.10 = (f32[64,128]{1,0:T(8,128)S(1)}, f32[64,128]{1,0:T(8,128)S(1)}, u32[]{:S(2)}, u32[]{:S(2)}) collective-permute-start(f32[64,128]{1,0:T(8,128)S(1)} %collective-permute-done.8.refs_1_), channel_id=1, source_target_pairs={{0,48},{1,49},{2,50},{3,51},{4,52},{5,53},{6,54},{7,55},{8,56},{9,... | collective-permute-start | bytes 98312 | tf_op jit(solution)/shard_map/ppermute | solution.py:23
  34.6 5.3 %collective-permute-start.9 = (f32[64,128]{1,0:T(8,128)S(1)}, f32[64,128]{1,0:T(8,128)S(1)}, u32[]{:S(2)}, u32[]{:S(2)}) collective-permute-start(f32[64,128]{1,0:T(8,128)S(1)} %maximum_maximum_fusion.refs_0_), channel_id=1, source_target_pairs={{0,48},{1,49},{2,50},{3,51},{4,52},{5,53},{6,54},{7,55},{8,56},{9,... | collective-permute-start | bytes 98312 | tf_op jit(solution)/shard_map/ppermute | solution.py:23
  35.3 5.1 %collective-permute-start.14 = (f32[64,128]{1,0:T(8,128)S(1)}, f32[64,128]{1,0:T(8,128)S(1)}, u32[]{:S(2)}, u32[]{:S(2)}) collective-permute-start(f32[64,128]{1,0:T(8,128)S(1)} %collective-permute-done.8.refs_1_), channel_id=1, source_target_pairs={{0,16},{1,17},{2,18},{3,19},{4,20},{5,21},{6,22},{7,23},{8,24},{9,... | collective-permute-start | bytes 98312 | tf_op jit(solution)/shard_map/ppermute | solution.py:23
  36.6 5.1 %collective-permute-start.12 = (f32[64,128]{1,0:T(8,128)S(1)}, f32[64,128]{1,0:T(8,128)S(1)}, u32[]{:S(2)}, u32[]{:S(2)}) collective-permute-start(f32[64,128]{1,0:T(8,128)S(1)} %collective-permute-done.11.refs_6_), channel_id=1, source_target_pairs={{0,16},{1,17},{2,18},{3,19},{4,20},{5,21},{6,22},{7,23},{8,24},{9,... | collective-permute-start | bytes 98312 | tf_op jit(solution)/shard_map/ppermute | solution.py:23
  36.6 5.1 %collective-permute-start.13 = (f32[64,128]{1,0:T(8,128)S(1)}, f32[64,128]{1,0:T(8,128)S(1)}, u32[]{:S(2)}, u32[]{:S(2)}) collective-permute-start(f32[64,128]{1,0:T(8,128)S(1)} %collective-permute-done.10.refs_3_), channel_id=1, source_target_pairs={{0,48},{1,49},{2,50},{3,51},{4,52},{5,53},{6,54},{7,55},{8,56},{9,... | collective-permute-start | bytes 98312 | tf_op jit(solution)/shard_map/ppermute | solution.py:23
  42.4 7.7 %collective-permute-start.15 = (f32[64,512]{1,0:T(8,128)S(1)}, f32[64,512]{1,0:T(8,128)S(1)}, u32[]{:S(2)}, u32[]{:S(2)}) collective-permute-start(f32[64,512]{1,0:T(8,128)S(1)} %get-tuple-element.12), channel_id=1, source_target_pairs={{0,12},{1,13},{2,14},{3,15},{4,0},{5,1},{6,2},{7,3},{8,4},{9,5},{1... | collective-permute-start | bytes 393224 | tf_op jit(solution)/shard_map/ppermute | solution.py:23
  46.2 6.6 %collective-permute-start.16 = (f32[64,512]{1,0:T(8,128)S(1)}, f32[64,512]{1,0:T(8,128)S(1)}, u32[]{:S(2)}, u32[]{:S(2)}) collective-permute-start(f32[64,512]{1,0:T(8,128)S(1)} %get-tuple-element.12), channel_id=1, source_target_pairs={{0,8},{1,9},{2,10},{3,11},{4,12},{5,13},{6,14},{7,15},{8,0},{9,1},... | collective-permute-start | bytes 393224 | tf_op jit(solution)/shard_map/ppermute | solution.py:23
  46.2 7.6 %collective-permute-start.17 = (f32[64,512]{1,0:T(8,128)S(1)}, f32[64,512]{1,0:T(8,128)S(1)}, u32[]{:S(2)}, u32[]{:S(2)}) collective-permute-start(f32[64,512]{1,0:T(8,128)S(1)} %get-tuple-element.12), channel_id=1, source_target_pairs={{0,4},{1,5},{2,6},{3,7},{4,8},{5,9},{6,10},{7,11},{8,12},{9,13},{1... | collective-permute-start | bytes 393224 | tf_op jit(solution)/shard_map/ppermute | solution.py:23
  54.6 17.9 %collective-permute-start.18 = (f32[4,64,512]{2,1,0:T(8,128)}, f32[4,64,512]{2,1,0:T(8,128)}, u32[]{:S(2)}, u32[]{:S(2)}) collective-permute-start(f32[4,64,512]{2,1,0:T(8,128)} %pad_maximum_fusion.e0), channel_id=1, source_target_pairs={{0,2},{1,3},{2,0},{3,1},{4,6},{5,7},{6,4},{7,5},{8,10},{9,11},{10,... | collective-permute-start | bytes 1572872 | tf_op jit(solution)/shard_map/ppermute | solution.py:23
  56.1 16.4 %collective-permute-start.21 = (f32[64,1024]{1,0:T(8,128)}, f32[64,1024]{1,0:T(8,128)}, u32[]{:S(2)}, u32[]{:S(2)}) collective-permute-start(f32[64,1024]{1,0:T(8,128)} %refs_0_.1), channel_id=1, source_target_pairs={{0,64},{1,65},{2,66},{3,67},{4,68},{5,69},{6,70},{7,71},{8,72},{9,... | collective-permute-start | bytes 786440 | tf_op jit(solution)/shard_map/ppermute | solution.py:23
  58.8 36.5 %collective-permute-start.24 = (f32[64,1024]{1,0:T(8,128)}, f32[64,1024]{1,0:T(8,128)}, u32[]{:S(2)}, u32[]{:S(2)}) collective-permute-start(f32[64,1024]{1,0:T(8,128)} %refs_0_.1), channel_id=1, source_target_pairs={{0,16},{1,17},{2,18},{3,19},{4,20},{5,21},{6,22},{7,23},{8,24},{9,... | collective-permute-start | bytes 786440 | tf_op jit(solution)/shard_map/ppermute | solution.py:23
  59.0 48.9 %collective-permute-start.22 = (f32[64,1024]{1,0:T(8,128)}, f32[64,1024]{1,0:T(8,128)}, u32[]{:S(2)}, u32[]{:S(2)}) collective-permute-start(f32[64,1024]{1,0:T(8,128)} %refs_0_.1), channel_id=1, source_target_pairs={{0,48},{1,49},{2,50},{3,51},{4,52},{5,53},{6,54},{7,55},{8,56},{9,... | collective-permute-start | bytes 786440 | tf_op jit(solution)/shard_map/ppermute | solution.py:23
  72.5 26.1 %collective-permute-start.19 = (f32[4,64,512]{2,1,0:T(8,128)}, f32[4,64,512]{2,1,0:T(8,128)}, u32[]{:S(2)}, u32[]{:S(2)}) collective-permute-start(f32[4,64,512]{2,1,0:T(8,128)} %pad_maximum_fusion.e0), channel_id=1, source_target_pairs={{0,1},{1,0},{2,3},{3,2},{4,5},{5,4},{6,7},{7,6},{8,9},{9,8},{10,11... | collective-permute-start | bytes 1572872 | tf_op jit(solution)/shard_map/ppermute | solution.py:23
  72.5 24.6 %collective-permute-start.23 = (f32[64,1024]{1,0:T(8,128)}, f32[64,1024]{1,0:T(8,128)}, u32[]{:S(2)}, u32[]{:S(2)}) collective-permute-start(f32[64,1024]{1,0:T(8,128)} %collective-permute-done.21.refs_1_), channel_id=1, source_target_pairs={{0,48},{1,49},{2,50},{3,51},{4,52},{5,53},{6,54},{7,55},{8,56},{9,... | collective-permute-start | bytes 786440 | tf_op jit(solution)/shard_map/ppermute | solution.py:23
  75.5 1.2 copy-start.5
  76.6 23.7 %collective-permute-start.20 = (f32[4,64,512]{2,1,0:T(8,128)}, f32[4,64,512]{2,1,0:T(8,128)}, u32[]{:S(2)}, u32[]{:S(2)}) collective-permute-start(f32[4,64,512]{2,1,0:T(8,128)} %collective-permute-done.18.e1), channel_id=1, source_target_pairs={{0,1},{1,0},{2,3},{3,2},{4,5},{5,4},{6,7},{7,6},{8,9},{9,8},{10,11... | collective-permute-start | bytes 1572872 | tf_op jit(solution)/shard_map/ppermute | solution.py:23
  76.9 1.4 copy-start.3
  78.3 1.4 copy-start.6
  82.8 17.5 %all-to-all-start = ((f32[8,32,512]{2,1,0:T(8,128)}), f32[8,32,512]{2,1,0:T(8,128)}, u32[]{:S(2)}, u32[]{:S(2)}) async-start(f32[8,32,512]{2,1,0:T(8,128)} %broadcast_in_dim.19), calls=%async_computation | async-start | bytes 1048576 | tf_op jit(solution)/shard_map/all_to_all | solution.py:203
  95.4 16.1 %collective-permute-start.27 = (f32[64,1024]{1,0:T(8,128)}, f32[64,1024]{1,0:T(8,128)}, u32[]{:S(2)}, u32[]{:S(2)}) collective-permute-start(f32[64,1024]{1,0:T(8,128)} %collective-permute-done.21.refs_1_), channel_id=1, source_target_pairs={{0,16},{1,17},{2,18},{3,19},{4,20},{5,21},{6,22},{7,23},{8,24},{9,... | collective-permute-start | bytes 786440 | tf_op jit(solution)/shard_map/ppermute | solution.py:23
  97.1 14.4 %collective-permute-start.25 = (f32[64,1024]{1,0:T(8,128)}, f32[64,1024]{1,0:T(8,128)}, u32[]{:S(2)}, u32[]{:S(2)}) collective-permute-start(f32[64,1024]{1,0:T(8,128)} %collective-permute-done.24.refs_6_), channel_id=1, source_target_pairs={{0,16},{1,17},{2,18},{3,19},{4,20},{5,21},{6,22},{7,23},{8,24},{9,... | collective-permute-start | bytes 786440 | tf_op jit(solution)/shard_map/ppermute | solution.py:23
  98.6 13.0 %collective-permute-start.26 = (f32[64,1024]{1,0:T(8,128)}, f32[64,1024]{1,0:T(8,128)}, u32[]{:S(2)}, u32[]{:S(2)}) collective-permute-start(f32[64,1024]{1,0:T(8,128)} %collective-permute-done.23.refs_3_), channel_id=1, source_target_pairs={{0,48},{1,49},{2,50},{3,51},{4,52},{5,53},{6,54},{7,55},{8,56},{9,... | collective-permute-start | bytes 786440 | tf_op jit(solution)/shard_map/ppermute | solution.py:23
  100.3 5.3 %copy-start.12 = (f32[512,1024]{1,0:T(8,128)S(1)}, f32[512,1024]{1,0:T(8,128)}, u32[]{:S(2)}) copy-start(f32[512,1024]{1,0:T(8,128)} %fusion.11) | copy-start | bytes 6291460
  103.6 1.0 copy-start.4
  104.6 1.0 copy-start.7
  105.6 6.0 %copy-start.8 = (f32[64,1024]{1,0:T(8,128)S(1)}, f32[64,1024]{1,0:T(8,128)}, u32[]{:S(2)}) copy-start(f32[64,1024]{1,0:T(8,128)} %refs_0_.1) | copy-start | bytes 786436
  107.4 9.1 %copy-start.11 = (f32[512,1024]{1,0:T(8,128)}, f32[512,1024]{1,0:T(8,128)S(1)}, u32[]{:S(2)}) copy-start(f32[512,1024]{1,0:T(8,128)S(1)} %fusion.12) | copy-start | bytes 6291460
  107.6 9.0 %collective-permute-start.28 = (f32[64,1024]{1,0:T(8,128)S(1)}, f32[64,1024]{1,0:T(8,128)S(1)}, u32[]{:S(2)}, u32[]{:S(2)}) collective-permute-start(f32[64,1024]{1,0:T(8,128)S(1)} %get-tuple-element.28), channel_id=1, source_target_pairs={{0,16},{1,17},{2,18},{3,19},{4,20},{5,21},{6,22},{7,23},{8,24},{9,... | collective-permute-start | bytes 786440 | tf_op jit(solution)/shard_map/ppermute | solution.py:23
  107.9 8.6 %collective-permute-start.30 = (f32[64,1024]{1,0:T(8,128)S(1)}, f32[64,1024]{1,0:T(8,128)S(1)}, u32[]{:S(2)}, u32[]{:S(2)}) collective-permute-start(f32[64,1024]{1,0:T(8,128)S(1)} %get-tuple-element.29), channel_id=1, source_target_pairs={{0,48},{1,49},{2,50},{3,51},{4,52},{5,53},{6,54},{7,55},{8,56},{9,... | collective-permute-start | bytes 786440 | tf_op jit(solution)/shard_map/ppermute | solution.py:23
  113.6 1.3 copy-start.1
  117.4 14.0 %collective-permute-start.29 = (f32[2,64,1024]{2,1,0:T(8,128)}, f32[2,64,1024]{2,1,0:T(8,128)}, u32[]{:S(2)}, u32[]{:S(2)}) collective-permute-start(f32[2,64,1024]{2,1,0:T(8,128)} %pad_maximum_fusion.1), channel_id=1, source_target_pairs={{0,16},{1,17},{2,18},{3,19},{4,20},{5,21},{6,22},{7,23},{8,24},{9,... | collective-permute-start | bytes 1572872 | tf_op jit(solution)/shard_map/ppermute | solution.py:23
  118.5 13.0 %collective-permute-start.31 = (f32[2,64,1024]{2,1,0:T(8,128)}, f32[2,64,1024]{2,1,0:T(8,128)}, u32[]{:S(2)}, u32[]{:S(2)}) collective-permute-start(f32[2,64,1024]{2,1,0:T(8,128)} %pad_maximum_fusion.2), channel_id=1, source_target_pairs={{0,48},{1,49},{2,50},{3,51},{4,52},{5,53},{6,54},{7,55},{8,56},{9,... | collective-permute-start | bytes 1572872 | tf_op jit(solution)/shard_map/ppermute | solution.py:23
  123.2 22.8 %all-to-all-start.1 = ((f32[16,32,512]{2,1,0:T(8,128)}), f32[16,32,512]{2,1,0:T(8,128)}, u32[]{:S(2)}, u32[]{:S(2)}) async-start(f32[16,32,512]{2,1,0:T(8,128)} %copy-done.7), calls=%async_computation.1 | async-start | bytes 2097152 | tf_op jit(solution)/shard_map/all_to_all | solution.py:217
  133.7 15.1 %collective-permute-start.32 = (f32[64,1024]{1,0:T(8,128)}, f32[64,1024]{1,0:T(8,128)}, u32[]{:S(2)}, u32[]{:S(2)}) collective-permute-start(f32[64,1024]{1,0:T(8,128)} %get-tuple-element.24), channel_id=1, source_target_pairs={{0,64},{1,65},{2,66},{3,67},{4,68},{5,69},{6,70},{7,71},{8,72},{9,... | collective-permute-start | bytes 786440 | tf_op jit(solution)/shard_map/ppermute | solution.py:23
  (3 other events, 2.7 us)
